TPU v7x, 32 devices: a whole 2x2x4 slice. The times are simulated.
32 devices in a mesh: tm: 16 (over z, x, core), space: 2 (over y).
Axes of the slice: x: 2, y: 2, z: 4, core: 2. Of those that a mesh axis runs over, the one named last changes fastest.
Arguments:
- conv_input: bfloat16 [16, 12, 40, 256], P('tm', None, 'space'), may hold values from -6 to 6
- conv_out: bfloat16 [16, 12, 40, 256], P('tm', None, 'space'), may hold values from -20 to 20
- kernel: bfloat16 [3, 3, 3, 256, 256], replicated, may hold values from -0.078125 to 0.078125
- gain: float32 [256], replicated, may hold values from 0.25 to 1.75
- bias: float32 [256], replicated, may hold values from -4 to 4
- cotangent: bfloat16 [16, 12, 40, 256], P('tm', None, 'space'), may hold values from -7 to 7
Outputs:
- grad_input: bfloat16 [16, 12, 40, 256], P('tm', None, 'space')
- grad_kernel: float32 [3, 3, 3, 256, 256], P(None, None, None, None, 'space')
- grad_gain: float32 [256], replicated
- grad_bias: float32 [256], replicated
All inputs are finite; a program needn't handle non-finite values.
Results may differ from a plain program's by a relative error of at most 0.0075.
Values may be sent and summed in bfloat16 or wider, within the bound.
A program may use at most 64 MiB of HBM per device.

v0:
```python
import jax
import jax.numpy as jnp
from jax import lax
from jax.sharding import PartitionSpec as P

GROUPS = 32


epsilon = 1e-06


def shifted_2(x, axis, by):
    size = lax.axis_size(axis)
    pairs = [(i, i + by) for i in range(size) if 0 <= i + by < size]
    return lax.ppermute(x, axis, pairs)


def extended_2(cells, sides, width):
    for axis, dim in sides:
        count = lax.axis_size(axis)
        ends = count - 1
        head = lax.slice_in_dim(cells, 0, width, axis=dim)
        tail = lax.slice_in_dim(cells, cells.shape[dim] - width, cells.shape[dim], axis=dim)
        cells = jnp.concatenate(
            [
                lax.ppermute(tail, axis, [(i, (i + 1) % count) for i in range(ends)]),
                cells,
                lax.ppermute(head, axis, [((i + 1) % count, i) for i in range(ends)]),
            ],
            axis=dim,
        )
    return cells


def frame_shift(block, step):
    return shifted_2(block, "tm", step)


def return_shift(block, step):
    return shifted_2(block.astype(jnp.bfloat16), "tm", step).astype(block.dtype)


def shards(conv_input, conv_out, kernel, gain, bias, cotangent):
    frames, rows, cols, chans = conv_out.shape
    width = chans // GROUPS
    grouped = conv_out.astype(jnp.float32).reshape(frames, rows, cols, GROUPS, width)
    total, square = lax.psum(
        (jnp.sum(grouped, axis=(0, 1, 2, 4)), jnp.sum(grouped * grouped, axis=(0, 1, 2, 4))),
        ("tm", "space"),
    )
    count = frames * rows * cols * width * lax.axis_size("tm") * lax.axis_size("space")
    mean = total / count
    inv_std = lax.rsqrt(square / count - mean * mean + epsilon)
    normed_grouped = (grouped - mean[:, None]) * inv_std[:, None]
    normed = normed_grouped.reshape(frames, rows, cols, chans)
    shifted = normed * gain + bias
    sigma = jax.nn.sigmoid(shifted)
    grad_shift = cotangent.astype(jnp.float32) * sigma * (1.0 + shifted * (1.0 - sigma))
    grad_grouped = (grad_shift * gain).reshape(frames, rows, cols, GROUPS, width)
    chan_bias, chan_gain = lax.psum(
        (jnp.sum(grad_shift, axis=(0, 1, 2)), jnp.sum(grad_shift * normed, axis=(0, 1, 2))),
        ("tm", "space"),
    )
    plain = jnp.sum((chan_bias * gain).reshape(GROUPS, width), axis=1)
    product = jnp.sum((chan_gain * gain).reshape(GROUPS, width), axis=1)
    grad_conv = inv_std[:, None] * (
        grad_grouped - plain[:, None] / count - normed_grouped * product[:, None] / count
    )
    grad_conv = grad_conv.reshape(frames, rows, cols, chans).astype(jnp.bfloat16)
    reach = 2
    earlier = [frame_shift(conv_input, step) for step in range(reach, 0, -1)]
    extended = jnp.concatenate(earlier + [conv_input], axis=0)
    whole_inputs = lax.all_gather(extended, "space", axis=2, tiled=True)
    channel_grads = lax.all_to_all(grad_conv, "space", split_axis=3, concat_axis=2, tiled=True)
    padded_inputs = jnp.pad(whole_inputs, ((0, 0), (1, 1), (1, 1), (0, 0)))
    wide = channel_grads.shape[2]
    contract = (((0, 1, 2), (0, 1, 2)), ((), ()))
    taps = []
    for tap_t in range(3):
        for tap_h in range(3):
            for tap_w in range(3):
                source = padded_inputs[
                    tap_t : tap_t + frames, tap_h : tap_h + rows, tap_w : tap_w + wide
                ]
                taps.append(
                    lax.dot_general(
                        source, channel_grads, contract, preferred_element_type=jnp.float32
                    )
                )
    local_kernel = jnp.stack(taps).reshape(3, 3, 3, chans, channel_grads.shape[3])
    rimmed = extended_2(grad_conv, (("space", 2),), 1)
    padded = jnp.pad(rimmed, ((0, 0), (1, 1), (0, 0), (0, 0)))
    transpose = (((3,), (1,)), ((), ()))
    partial_sums = jnp.zeros((frames + 2, rows, cols, chans), jnp.float32)
    for tap_t in range(3):
        section = jnp.zeros((frames, rows, cols, chans), jnp.float32)
        for tap_h in range(3):
            for tap_w in range(3):
                window = padded[:, 2 - tap_h : 2 - tap_h + rows, 2 - tap_w : 2 - tap_w + cols]
                section = section + lax.dot_general(
                    window,
                    kernel[tap_t, tap_h, tap_w],
                    transpose,
                    preferred_element_type=jnp.float32,
                )
        partial_sums = partial_sums.at[tap_t : tap_t + frames].add(section)
    local_part = partial_sums[2:]
    local_part = (
        local_part + return_shift(partial_sums[0:1], -2) + return_shift(partial_sums[1:2], -1)
    )
    grad_input = local_part.astype(jnp.bfloat16)
    grad_kernel = lax.psum(local_kernel, "tm")
    return (grad_input, grad_kernel, chan_gain, chan_bias)


def solution(mesh):
    return jax.shard_map(
        shards,
        mesh=mesh,
        in_specs=(
            P("tm", None, "space", None),
            P("tm", None, "space", None),
            P(),
            P(),
            P(),
            P("tm", None, "space", None),
        ),
        out_specs=(P("tm", None, "space", None), P(None, None, None, None, "space"), P(), P()),
        check_vma=False,
    )
```

profile of v0, /device:TPU:0, one launch (start us, length us, event | category | flops | bytes accessed | tf_op | source)
XLA Modules:
  0.0 271.4 jit_solution(3972550199970189502)
XLA Ops:
  7.2 0.9 copy.12
  8.1 2.4 collective-permute-start.5
  10.5 1.0 fusion.39
  11.9 4.4 %collective-permute-start.4 = (bf16[1,12,20,256]{3,1,0,2:T(8,128)(2,1)S(1)}, bf16[1,12,20,256]{3,1,0,2:T(8,128)(2,1)S(1)}, u32[]{:S(2)}, u32[]{:S(2)}) collective-permute-start(bf16[1,12,20,256]{3,1,0,2:T(8,128)(2,1)S(1)} %copy.12), channel_id=1, source_target_pairs={{0,4},{2,6},{4,8},{6,10},{8,12},{10,14},{12,16},{14,18},{16,20},{1... | collective-permute-start | bytes 368648 | tf_op jit(solution)/shard_map/ppermute | solution.py:15
  16.3 40.7 %all-reduce.3 = (f32[32]{0:T(128)S(1)}, f32[32]{0:T(128)S(1)}) all-reduce(f32[32]{0:T(128)S(1)} %reduce_sum.73, f32[32]{0:T(128)S(1)} %reduce_sum.70), channel_id=1, replica_groups=mesh['tm'=16,'space'=2] {'tm','space'}, use_global_device_ids=true, to_apply=%region_5.0 | all-reduce | flops 64 | bytes 512 | tf_op jit(solution)/shard_map/psum | solution.py:47
  57.4 1.2 fusion.214
  58.6 39.8 %all-reduce.2 = (f32[256]{0:T(256)S(1)}, f32[256]{0:T(256)S(1)}) all-reduce(f32[256]{0:T(256)S(1)} %get-tuple-element.41, f32[256]{0:T(256)S(1)} %get-tuple-element.40), channel_id=1, replica_groups=mesh['tm'=16,'space'=2] {'tm','space'}, use_global_device_ids=true, to_apply=%region_10.11 | all-reduce | flops 512 | bytes 4096 | tf_op jit(solution)/shard_map/psum | solution.py:60
  98.4 0.7 fusion.217
  99.8 1.0 fusion.56
  100.9 4.2 %collective-permute-start = (bf16[1,12,1,256]{3,2,1,0:T(2,128)(2,1)S(1)}, bf16[1,12,1,256]{3,2,1,0:T(2,128)(2,1)S(1)}, u32[]{:S(2)}, u32[]{:S(2)}) collective-permute-start(bf16[1,12,1,256]{3,2,1,0:T(2,128)(2,1)S(1)} %get-tuple-element.49), channel_id=1, source_target_pairs={{0,1},{2,3},{4,5},{6,7},{8,9},{10,11},{12,13},{14,15},{16,17},{18,... | collective-permute-start | bytes 18440 | tf_op jit(solution)/shard_map/ppermute | solution.py:26
  105.1 1.3 collective-permute-start.1
  106.4 1.0 copy.16
  107.4 1.8 reshape.522
  109.1 3.9 %all-to-all-start = ((bf16[2,2,15360]{2,1,0:T(2,128)(2,1)}), bf16[2,2,15360]{2,1,0:T(2,128)(2,1)S(1)}, u32[]{:S(2)}, u32[]{:S(2)}) async-start(bf16[2,2,15360]{2,1,0:T(2,128)(2,1)} %reshape.522), calls=%async_computation | async-start | bytes 245760 | tf_op jit(solution)/shard_map/all_to_all | solution.py:74
  113.1 1.3 fusion.114
  114.3 1.1 fusion.112
  115.5 1.1 fusion.116
  116.7 1.1 fusion.131
  117.9 1.1 fusion.120
  119.0 1.1 fusion.138
  121.6 0.2 fusion.3
  122.5 1.3 collective-permute-start.2
  124.8 1.3 collective-permute-start.3
  126.1 1.1 reshape.523
  127.3 0.8 copy.17
  128.2 14.7 %all_gather.3 = bf16[3,12,40,256]{3,1,0,2:T(8,128)(2,1)S(1)} all-gather(bf16[3,12,20,256]{3,1,0,2:T(8,128)(2,1)S(1)} %pad_maximum_fusion), channel_id=1, replica_groups=mesh['tm'=16,'space'=2] {'space'}, dimensions={2}, use_global_device_ids=true | all-gather | bytes 1105920 | tf_op jit(solution)/shard_map/all_gather | solution.py:73
  143.1 0.3 fusion.37
  143.3 0.3 fusion.36
  143.6 0.3 fusion.35
  143.8 0.3 fusion.34
  144.1 0.3 fusion.33
  144.4 0.3 fusion.32
  144.6 0.3 fusion.31
  144.9 0.3 fusion.30
  145.2 0.3 fusion.29
  145.4 0.3 fusion.28
  145.7 0.3 fusion.27
  146.0 0.3 fusion.26
  146.2 0.3 fusion.25
  146.5 0.3 fusion.24
  146.8 0.3 fusion.23
  147.0 0.3 fusion.22
  147.3 0.3 fusion.21
  147.6 0.3 fusion.20
  147.8 0.3 fusion.19
  148.1 0.3 fusion.18
  148.4 0.3 fusion.17
  148.6 0.3 fusion.16
  148.9 0.3 fusion.15
  149.2 0.3 fusion.14
  149.4 0.3 fusion.13
  149.7 0.3 fusion.12
  150.0 0.3 fusion.11
  150.2 1.8 copy-done
  152.0 1.1 fusion.149
  153.2 1.1 convolution_add_fusion.17
  154.3 1.1 convolution_add_fusion.16
  155.5 1.1 fusion.6
  156.6 1.1 fusion.5
  157.8 1.1 convolution_add_fusion.13
  158.9 1.2 fusion.4
  160.1 0.7 add_convert_fusion
  160.8 99.6 %all-reduce.6.cloned.1.call-done = f32[3,3,3,256,128]{4,3,2,1,0:T(8,128)} async-done(((f32[3,3,3,256,128]{4,3,2,1,0:T(8,128)}), f32[3,3,3,256,128]{4,3,2,1,0:T(8,128)}) %all-reduce.6.cloned.1.call-update) | async-done | bytes 3538960 | tf_op jit(solution)/shard_map/psum | solution.py:112
  260.4 4.2 %copy.48 = f32[3,3,3,256,128]{4,3,2,1,0:T(8,128)} copy(f32[3,3,3,256,128]{4,3,2,1,0:T(8,128)} %all-reduce.6.cloned.1.call-done) | data formatting | bytes 7077888
  (52 shorter events, 5.0 us)
Async XLA Ops:
  8.1 120.0 %collective-permute-start.5 = (bf16[1,12,20,256]{3,1,0,2:T(8,128)(2,1)S(1)}, bf16[1,12,20,256]{3,1,0,2:T(8,128)(2,1)S(1)}, u32[]{:S(2)}, u32[]{:S(2)}) collective-permute-start(bf16[1,12,20,256]{3,1,0,2:T(8,128)(2,1)S(1)} %copy.12), channel_id=1, source_target_pairs={{0,2},{2,4},{4,6},{6,8},{8,10},{10,12},{12,14},{14,16},{16,18},{18... | collective-permute-start | bytes 368648 | tf_op jit(solution)/shard_map/ppermute | solution.py:15
  11.9 116.2 %collective-permute-start.4 = (bf16[1,12,20,256]{3,1,0,2:T(8,128)(2,1)S(1)}, bf16[1,12,20,256]{3,1,0,2:T(8,128)(2,1)S(1)}, u32[]{:S(2)}, u32[]{:S(2)}) collective-permute-start(bf16[1,12,20,256]{3,1,0,2:T(8,128)(2,1)S(1)} %copy.12), channel_id=1, source_target_pairs={{0,4},{2,6},{4,8},{6,10},{8,12},{10,14},{12,16},{14,18},{16,20},{1... | collective-permute-start | bytes 368648 | tf_op jit(solution)/shard_map/ppermute | solution.py:15
  98.4 21.8 %copy-start.2 = (f32[256]{0:T(256)}, f32[256]{0:T(256)S(1)}, u32[]{:S(2)}) copy-start(f32[256]{0:T(256)S(1)} %get-tuple-element.57) | copy-start | bytes 3076
  98.4 21.8 %copy-start.3 = (f32[256]{0:T(256)}, f32[256]{0:T(256)S(1)}, u32[]{:S(2)}) copy-start(f32[256]{0:T(256)S(1)} %get-tuple-element.58) | copy-start | bytes 3076
  100.9 15.7 %collective-permute-start = (bf16[1,12,1,256]{3,2,1,0:T(2,128)(2,1)S(1)}, bf16[1,12,1,256]{3,2,1,0:T(2,128)(2,1)S(1)}, u32[]{:S(2)}, u32[]{:S(2)}) collective-permute-start(bf16[1,12,1,256]{3,2,1,0:T(2,128)(2,1)S(1)} %get-tuple-element.49), channel_id=1, source_target_pairs={{0,1},{2,3},{4,5},{6,7},{8,9},{10,11},{12,13},{14,15},{16,17},{18,... | collective-permute-start | bytes 18440 | tf_op jit(solution)/shard_map/ppermute | solution.py:26
  105.1 11.6 %collective-permute-start.1 = (bf16[1,12,1,256]{3,2,1,0:T(2,128)(2,1)S(1)}, bf16[1,12,1,256]{3,2,1,0:T(2,128)(2,1)S(1)}, u32[]{:S(2)}, u32[]{:S(2)}) collective-permute-start(bf16[1,12,1,256]{3,2,1,0:T(2,128)(2,1)S(1)} %get-tuple-element.50), channel_id=1, source_target_pairs={{1,0},{3,2},{5,4},{7,6},{9,8},{11,10},{13,12},{15,14},{17,16},{19,... | collective-permute-start | bytes 18440 | tf_op jit(solution)/shard_map/ppermute | solution.py:28
  109.1 16.9 %all-to-all-start = ((bf16[2,2,15360]{2,1,0:T(2,128)(2,1)}), bf16[2,2,15360]{2,1,0:T(2,128)(2,1)S(1)}, u32[]{:S(2)}, u32[]{:S(2)}) async-start(bf16[2,2,15360]{2,1,0:T(2,128)(2,1)} %reshape.522), calls=%async_computation | async-start | bytes 245760 | tf_op jit(solution)/shard_map/all_to_all | solution.py:74
  113.1 147.4 %all-reduce.6.cloned.1.call-start = ((), (), s32[]{:S(2)}) async-start(), calls=%async_computation.1 | async-start | bytes 7077888 | tf_op jit(solution)/shard_map/psum | solution.py:112
  113.1 7.1 %copy-start.1 = (bf16[3,3,3,256,256]{4,3,2,1,0:T(8,128)(2,1)S(1)}, bf16[3,3,3,256,256]{4,3,2,1,0:T(8,128)(2,1)}, u32[]{:S(2)}) copy-start(bf16[3,3,3,256,256]{4,3,2,1,0:T(8,128)(2,1)} %param.14) | copy-start | bytes 10616836
  122.5 37.6 %collective-permute-start.2 = (bf16[1,12,20,256]{3,2,1,0:T(8,128)(2,1)S(1)}, bf16[1,12,20,256]{3,2,1,0:T(8,128)(2,1)S(1)}, u32[]{:S(2)}, u32[]{:S(2)}) collective-permute-start(bf16[1,12,20,256]{3,2,1,0:T(8,128)(2,1)S(1)} %fusion.10), channel_id=1, source_target_pairs={{4,0},{6,2},{8,4},{10,6},{12,8},{14,10},{16,12},{18,14},{20,16},{2... | collective-permute-start | bytes 368648 | tf_op jit(solution)/shard_map/ppermute | solution.py:15
  124.8 35.3 %collective-permute-start.3 = (bf16[1,12,20,256]{3,2,1,0:T(8,128)(2,1)S(1)}, bf16[1,12,20,256]{3,2,1,0:T(8,128)(2,1)S(1)}, u32[]{:S(2)}, u32[]{:S(2)}) collective-permute-start(bf16[1,12,20,256]{3,2,1,0:T(8,128)(2,1)S(1)} %fusion.9), channel_id=1, source_target_pairs={{2,0},{4,2},{6,4},{8,6},{10,8},{12,10},{14,12},{16,14},{18,16},{20... | collective-permute-start | bytes 368648 | tf_op jit(solution)/shard_map/ppermute | solution.py:15
  150.2 1.8 copy-start
Sparse Core Ops, SparseCore 0:
  152.2 108.2 all-reduce.5
where the time goes:
time: 272 us; the launch traced here: 271 us
  waiting for transfers between devices  99.6 us (37%)
  blocking collectives  95.2 us (35%)
  matrix products  25.2 us (9%)
  starting transfers between devices  18.8 us (7%)
  between operations  14.5 us (5%)
  local copies, waits for them, and re-layouts  12.9 us (5%)
  other arithmetic  5.27 us (2%)
    psum x1, waiting for transfers between devices, shards(): grad_kernel = lax.psum(local_kernel, 'tm')  99.6 us
    psum x1, blocking collectives, shards(): lax.psum((jnp.sum(grouped, axis=(0, 1, 2, 4)), jnp.sum(grouped * grouped,...  40.7 us
    psum x1, blocking collectives, shards(): lax.psum((jnp.sum(grad_shift, axis=(0, 1, 2)), jnp.sum(grad_shift * norme...  39.8 us
    dot_general x27, matrix products, shards(): lax.dot_general(window, kernel[tap_t, tap_h, tap_w], transpose, preferred...  18.1 us
    all_gather x1, blocking collectives, shards(): whole_inputs = lax.all_gather(extended, 'space', axis=2, tiled=True)  14.7 us
    unnamed x12, local copies, waits for them, and re-layouts  9.84 us
    ppermute x4, starting transfers between devices, shifted_2(): return lax.ppermute(x, axis, pairs)  9.39 us
    dot_general x27, matrix products, shards(): lax.dot_general(source, channel_grads, contract, preferred_element_type=j...  7.09 us
  transfers between devices with their start and end apart: 8, of which 1 were waited for; matrix products, arithmetic and copies ran while one was open for 13% of the time, Pallas kernels for 0%

commit v1 on v0

v1 whole, which is shorter than its diff:
```python
import functools

import jax
import jax.numpy as jnp
from jax import lax
from jax.experimental import pallas as pl
from jax.experimental.pallas import tpu as pltpu
from jax.sharding import PartitionSpec as P

GROUPS = 32
EPSILON = 1e-06
MESH = pl.DeviceIdType.MESH
F32 = jnp.float32
BF16 = jnp.bfloat16


def round_up(value, unit):
    return (value + unit - 1) // unit * unit


def group_sum(x, width):
    lanes = x.shape[1]
    lane = lax.broadcasted_iota(jnp.int32, x.shape, 1)
    step = 1
    while step < width:
        up = pltpu.roll(x, lanes - step, 1)
        down = pltpu.roll(x, step, 1)
        x = x + jnp.where((lane // step) % 2 == 0, up, down)
        step *= 2
    return x


def body(
    T, S, total_rows,
    x_ref, co_ref, k_ref, gain_ref, bias_ref, ct_ref,
    gi_ref, gk_ref, gg_ref, gb_ref,
    strip, edge_out, edge_in, slice_out, slice_in, x_in,
    st_out, st_in, fbuf, gown, gwide, xt, wbuf, acc, sbuf, rbuf,
    w_sem, st_send, st_recv, bulk_send, bulk_recv, rs_send, rs_recv,
):
    N = T * S
    _, rows, cols, chans = co_ref.shape
    ce = chans // S
    pitch = fbuf.shape[1]
    flat = rows * pitch
    flat_all = (rows + 2) * pitch
    halves = chans // 128
    t = lax.axis_index("tm")
    s = lax.axis_index("space")
    me = t * S + s

    load = pltpu.make_async_copy(k_ref, wbuf, w_sem)
    load.start()

    barrier = pltpu.get_barrier_semaphore()

    def greet(r, carry):
        d = lax.rem(me + r, N)
        pl.semaphore_signal(barrier, inc=1, device_id=(d // S, lax.rem(d, S)), device_id_type=MESH)
        return carry

    lax.fori_loop(1, N, greet, 0)

    for arr, ref in ((0, co_ref), (1, ct_ref)):
        whole = ref[0]
        for h in range(rows):
            edge_out[0, arr, h : h + 1, :] = whole[h, 0:1, :]
            edge_out[1, arr, h : h + 1, :] = whole[h, cols - 1 : cols, :]
        for j in range(S):
            slice_out[j, arr] = whole[:, :, j * ce : (j + 1) * ce]
    conv = co_ref[0].astype(F32)
    first = jnp.sum(jnp.sum(conv, axis=0), axis=0, keepdims=True)
    second = jnp.sum(jnp.sum(conv * conv, axis=0), axis=0, keepdims=True)

    def put_stats(which, one, two):
        for i in range(halves):
            st_out[which, i : i + 1, :] = one[:, i * 128 : (i + 1) * 128]
            st_out[which, halves + i : halves + i + 1, :] = two[:, i * 128 : (i + 1) * 128]

    def send_stats(which):
        def send(r, carry):
            d = lax.rem(me + r, N)
            pltpu.make_async_remote_copy(
                src_ref=st_out.at[which], dst_ref=st_in.at[which, r - 1],
                send_sem=st_send.at[which], recv_sem=st_recv.at[which],
                device_id=(d // S, lax.rem(d, S)), device_id_type=MESH,
            ).start()
            return carry

        lax.fori_loop(1, N, send, 0)

    def take_stats(which):
        pltpu.make_async_copy(st_in.at[which], st_in.at[which], st_recv.at[which]).wait()
        return jnp.sum(st_in[which], axis=0) + st_out[which]

    put_stats(0, first, second)
    pl.semaphore_wait(barrier, N - 1)
    send_stats(0)

    bulk = []

    def push(src, dst, device):
        i = len(bulk)
        copy = pltpu.make_async_remote_copy(
            src_ref=src, dst_ref=dst, send_sem=bulk_send.at[i], recv_sem=bulk_recv.at[i],
            device_id=device, device_id_type=MESH,
        )
        copy.start()
        bulk.append(copy)

    for k in range(3):
        tk = lax.rem(t + T - k, T)
        push(edge_out.at[1], edge_in.at[k, 0], (tk, lax.rem(s + 1, S)))
        push(edge_out.at[0], edge_in.at[k, 1], (tk, lax.rem(s + S - 1, S)))
        for r in range(1, S):
            other = lax.rem(s + S - r, S)
            push(slice_out.at[other], slice_in.at[k, r - 1], (tk, other))
    for r in range(1, S):
        push(x_ref.at[0], x_in.at[r - 1], (t, lax.rem(s + S - r, S)))
    for k in range(1, 3):
        tk = lax.rem(t + T - k, T)
        push(co_ref.at[0], strip.at[k - 1, 0], (tk, s))
        push(ct_ref.at[0], strip.at[k - 1, 1], (tk, s))

    fbuf[...] = jnp.zeros_like(fbuf)

    def put_input(index, value):
        fbuf[1 : rows + 1, 0:cols, :] = value.astype(F32)
        placed = fbuf[1 : rows + 1].reshape(flat, chans)
        xt[index] = jnp.transpose(placed).astype(BF16)

    put_input(0, x_ref[0])
    if total_rows > 27 * chans:
        acc[27 * chans :, :] = jnp.zeros((total_rows - 27 * chans, ce), F32)

    gain = gain_ref[...]
    bias = bias_ref[...]
    width = chans // GROUPS
    count = rows * cols * width * N
    sums = take_stats(0)
    grouped = group_sum(sums, width)
    mean2 = grouped[:halves] / count
    inv2 = lax.rsqrt(grouped[halves:] / count - mean2 * mean2 + EPSILON)

    def wide(two):
        return jnp.concatenate([two[i : i + 1] for i in range(halves)], axis=1)

    mean, inv = wide(mean2), wide(inv2)

    def shift_grad(conv, cot, mean, inv, gain, bias):
        normed = (conv.astype(F32) - mean) * inv
        shifted = normed * gain + bias
        sigma = jax.nn.sigmoid(shifted)
        return normed, cot.astype(F32) * sigma * (1.0 + shifted * (1.0 - sigma))

    normed, grad = shift_grad(co_ref[0], ct_ref[0], mean, inv, gain, bias)
    put_stats(
        1,
        jnp.sum(jnp.sum(grad, axis=0), axis=0, keepdims=True),
        jnp.sum(jnp.sum(grad * normed, axis=0), axis=0, keepdims=True),
    )
    send_stats(1)
    for copy in bulk:
        copy.wait_recv()
    for r in range(1, S):
        put_input(r, x_in[r - 1])
    sums = take_stats(1)
    chan_bias, chan_gain = wide(sums[:halves]), wide(sums[halves:])
    gb_ref[...] = chan_bias
    gg_ref[...] = chan_gain
    gain2 = jnp.concatenate([gain[:, i * 128 : (i + 1) * 128] for i in range(halves)], axis=0)
    plain = wide(group_sum(sums[:halves] * gain2, width)) / count
    product = wide(group_sum(sums[halves:] * gain2, width)) / count

    def conv_grad(conv, cot, params):
        mean, inv, gain, bias, plain, product = params
        normed, grad = shift_grad(conv, cot, mean, inv, gain, bias)
        return inv * (grad * gain - plain - normed * product)

    def part(v):
        out = v[..., 0:ce]
        for j in range(1, S):
            out = jnp.where(s == j, v[..., j * ce : (j + 1) * ce], out)
        return out

    params = (mean, inv, gain, bias, plain, product)
    own_params = tuple(part(p) for p in params)

    def shifts(f):
        n = f.shape[0]
        return (pltpu.roll(f, n - 1, 0), f, pltpu.roll(f, 1, 0))

    for k in range(3):
        live = t + k < T
        conv, cot = (co_ref[0], ct_ref[0]) if k == 0 else (strip[k - 1, 0], strip[k - 1, 1])
        g = jnp.where(live, conv_grad(conv, cot, params), 0.0)
        fbuf[1 : rows + 1, 0:cols, :] = g
        left = jnp.where(live & (s > 0), conv_grad(edge_in[k, 0, 0], edge_in[k, 0, 1], params), 0.0)
        right = jnp.where(live & (s < S - 1), conv_grad(edge_in[k, 1, 0], edge_in[k, 1, 1], params), 0.0)
        for h in range(rows):
            fbuf[h, pitch - 1 : pitch, :] = left[h : h + 1]
            fbuf[h + 1, cols : cols + 1, :] = right[h : h + 1]
        f = fbuf[...].reshape(flat_all, chans)
        for c, w in enumerate(shifts(f)):
            gown[k, :, c * chans : (c + 1) * chans] = w.astype(BF16)
            gwide[0, k, :, c * ce : (c + 1) * ce] = part(w).astype(BF16)
        near = [part(g)] + [
            jnp.where(live, conv_grad(slice_in[k, r - 1, 0], slice_in[k, r - 1, 1], own_params), 0.0)
            for r in range(1, S)
        ]
        for r in range(1, S):
            j = lax.rem(s + r, S)
            before, after = near[r - 1], near[(r + 1) % S]
            fbuf[1 : rows + 1, 0:cols, 0:ce] = near[r]
            fbuf[0:rows, pitch - 1 : pitch, 0:ce] = jnp.where(j > 0, before[:, cols - 1 : cols, :], 0.0)
            fbuf[1 : rows + 1, cols : cols + 1, 0:ce] = jnp.where(j < S - 1, after[:, 0:1, :], 0.0)
            f = fbuf[:, :, 0:ce].reshape(flat_all, ce)
            for c, w in enumerate(shifts(f)):
                gwide[r, k, :, c * ce : (c + 1) * ce] = w.astype(BF16)

    for a in range(3):
        for b in range(3):
            res = None
            for j in range(S):
                term = jnp.dot(
                    xt[j], gwide[j, 2 - a, (2 - b) * pitch : (2 - b) * pitch + flat, :],
                    preferred_element_type=F32,
                )
                res = term if res is None else res + term
            for c in range(3):
                at = ((a * 3 + b) * 3 + c) * chans
                acc[at : at + chans, :] = res[:, c * ce : (c + 1) * ce]

    bits = T.bit_length() - 1
    orders = [list(range(bits)), list(range(bits))]
    if bits > 2:
        orders[1][1], orders[1][2] = orders[1][2], orders[1][1]
    size = total_rows // 2
    offs = [0, 0]
    where = 0
    copies = []

    def side(bit):
        return lax.rem(t // (2**bit), 2)

    def partner(bit):
        return (t + (1 - 2 * side(bit)) * 2**bit, s)

    def span(p, off, n):
        return pl.ds(pl.multiple_of(p * size + off, 16), n)

    def begin(i, p):
        half = size >> (i + 1)
        start = size - (size >> i)
        bit = orders[p][i]
        mine = side(bit)
        sbuf[p, start : start + half, :] = acc[span(p, offs[p] + (1 - mine) * half, half), :].astype(BF16)
        copy = pltpu.make_async_remote_copy(
            src_ref=sbuf.at[p, start : start + half], dst_ref=rbuf.at[p, start : start + half],
            send_sem=rs_send.at[0, p, i], recv_sem=rs_recv.at[0, p, i],
            device_id=partner(bit), device_id_type=MESH,
        )
        copy.start()
        copies.append(copy)
        offs[p] = offs[p] + mine * half
        return copy

    def finish(i, p, copy):
        half = size >> (i + 1)
        start = size - (size >> i)
        copy.wait_recv()
        at = span(p, offs[p], half)
        acc[at, :] = acc[at, :] + rbuf[p, start : start + half, :].astype(F32)

    def input_grad(taps):
        total = None
        for a, b, c in taps:
            term = lax.dot_general(
                gown[2 - a, (2 - b) * pitch : (2 - b) * pitch + flat, c * chans : (c + 1) * chans],
                wbuf[a, b, c], (((1,), (1,)), ((), ())), preferred_element_type=F32,
            )
            total = term if total is None else total + term
        return total

    flying = [begin(0, 0), begin(0, 1)]
    for i in range(bits):
        for p in range(2):
            finish(i, p, flying[p])
            if i + 1 < bits:
                flying[p] = begin(i + 1, p)
        if i == 0:
            load.wait()
            every = [(a, b, c) for a in range(3) for b in range(3) for c in range(3)]
            total = input_grad(every).reshape(rows, pitch, chans)
            gi_ref[0] = total[:, 0:cols, :].astype(BF16)
    block = size >> bits
    for p in range(2):
        at = span(p, offs[p], block)
        gk_ref[at, :] = acc[at, :].astype(BF16)

    def spread(i, p):
        n = size >> (i + 1)
        bit = orders[p][i]
        at = span(p, offs[p], n)
        copy = pltpu.make_async_remote_copy(
            src_ref=gk_ref.at[at], dst_ref=gk_ref.at[at],
            send_sem=rs_send.at[1, p, i], recv_sem=rs_recv.at[1, p, i],
            device_id=partner(bit), device_id_type=MESH,
        )
        copy.start()
        copies.append(copy)
        offs[p] = offs[p] - side(bit) * n
        return copy

    flying = [spread(bits - 1, 0), spread(bits - 1, 1)]
    for i in reversed(range(bits)):
        for p in range(2):
            flying[p].wait_recv()
            if i > 0:
                flying[p] = spread(i - 1, p)

    for copy in copies:
        copy.wait_send()
    for copy in bulk:
        copy.wait_send()
    for which in range(2):
        pltpu.make_async_copy(st_in.at[which], st_in.at[which], st_send.at[which]).wait()


def solution(mesh):
    T, S = mesh.shape["tm"], mesh.shape["space"]

    def shards(conv_input, conv_out, kernel, gain, bias, cotangent):
        _, rows, cols, chans = conv_out.shape
        ce = chans // S
        bits = T.bit_length() - 1
        total_rows = round_up(27 * chans, 2 * T * 16)
        pitch = round_up(cols + 2, 16)
        n_bulk = 3 * (2 + S - 1) + (S - 1) + 4
        size = total_rows // 2
        vmem = pl.BlockSpec(memory_space=pltpu.VMEM)
        gi, gk, gg, gb = pl.pallas_call(
            functools.partial(body, T, S, total_rows),
            out_shape=(
                jax.ShapeDtypeStruct(conv_input.shape, BF16),
                jax.ShapeDtypeStruct((total_rows, ce), BF16),
                jax.ShapeDtypeStruct((1, chans), F32),
                jax.ShapeDtypeStruct((1, chans), F32),
            ),
            in_specs=[vmem, vmem, pl.BlockSpec(memory_space=pl.ANY), vmem, vmem, vmem],
            out_specs=(vmem, vmem, vmem, vmem),
            scratch_shapes=[
                pltpu.VMEM((2, 2, rows, cols, chans), BF16),
                pltpu.VMEM((2, 2, rows, chans), BF16),
                pltpu.VMEM((3, 2, 2, rows, chans), BF16),
                pltpu.VMEM((S, 2, rows, cols, ce), BF16),
                pltpu.VMEM((3, S - 1, 2, rows, cols, ce), BF16),
                pltpu.VMEM((S - 1, rows, cols, chans), BF16),
                pltpu.VMEM((2, 2 * chans // 128, 128), F32),
                pltpu.VMEM((2, T * S - 1, 2 * chans // 128, 128), F32),
                pltpu.VMEM((rows + 2, pitch, chans), F32),
                pltpu.VMEM((3, (rows + 2) * pitch, 3 * chans), BF16),
                pltpu.VMEM((S, 3, (rows + 2) * pitch, 3 * ce), BF16),
                pltpu.VMEM((S, chans, rows * pitch), BF16),
                pltpu.VMEM((3, 3, 3, chans, chans), BF16),
                pltpu.VMEM((total_rows, ce), F32),
                pltpu.VMEM((2, size, ce), BF16),
                pltpu.VMEM((2, size, ce), BF16),
                pltpu.SemaphoreType.DMA,
                pltpu.SemaphoreType.DMA((2,)),
                pltpu.SemaphoreType.DMA((2,)),
                pltpu.SemaphoreType.DMA((n_bulk,)),
                pltpu.SemaphoreType.DMA((n_bulk,)),
                pltpu.SemaphoreType.DMA((2, 2, bits)),
                pltpu.SemaphoreType.DMA((2, 2, bits)),
            ],
            compiler_params=pltpu.CompilerParams(
                collective_id=0, has_side_effects=True, vmem_limit_bytes=60 * 1024 * 1024
            ),
        )(conv_input, conv_out, kernel, gain.reshape(1, chans), bias.reshape(1, chans), cotangent)
        grad_kernel = gk[: 27 * chans].astype(F32).reshape(3, 3, 3, chans, ce)
        return gi, grad_kernel, gg.reshape(chans), gb.reshape(chans)

    strip = P("tm", None, "space", None)
    return jax.shard_map(
        shards,
        mesh=mesh,
        in_specs=(strip, strip, P(), P(), P(), strip),
        out_specs=(strip, P(None, None, None, None, "space"), P(), P()),
        check_vma=False,
    )
```

time: 272 us -> 76.1 us (0.28)
  waiting for transfers between devices: 99.6 us -> 0 us
  blocking collectives: 95.2 us -> 0 us
  Pallas kernels: 0 us -> 69.7 us
  matrix products: 25.2 us -> 0 us
  starting transfers between devices: 18.8 us -> 0 us
  between operations: 14.5 us -> 0.67 us
  local copies, waits for them, and re-layouts: 12.9 us -> 3.39 us
  other arithmetic: 5.27 us -> 2.19 us
    psum x1 -> x0, waiting for transfers between devices: 99.6 us -> none  [shards(): grad_kernel = lax.psum(local_kernel, 'tm')]
    psum x2 -> x0, blocking collectives: 80.5 us -> none  [the longest x1 40.7 us: shards(): lax.psum((jnp.sum(grouped, axis=(0, 1, 2, 4)), jnp.sum(grouped * grouped,...]
    pallas_call x0 -> x1, Pallas kernels: none -> 69.7 us  [shards(): pl.pallas_call(functools.partial(body, T, S, total_rows), out_shape=(jax....]
    dot_general x54 -> x0, matrix products: 25.2 us -> none  [the longest x27 18.1 us: shards(): lax.dot_general(window, kernel[tap_t, tap_h, tap_w], transpose, preferred...]
    ppermute x6 -> x0, starting transfers between devices: 14.9 us -> none  [the longest x4 9.39 us: shifted_2(): return lax.ppermute(x, axis, pairs)]
    all_gather x1 -> x0, blocking collectives: 14.7 us -> none  [shards(): whole_inputs = lax.all_gather(extended, 'space', axis=2, tiled=True)]
    unnamed x12 -> x9, local copies, waits for them, and re-layouts: 9.84 us -> 1.8 us
    all_to_all x1 -> x0, starting transfers between devices: 3.91 us -> none  [shards(): lax.all_to_all(grad_conv, 'space', split_axis=3, concat_axis=2, tiled=True)]
  transfers between devices with their start and end apart: 8 -> 0, of which waited for: 1 -> 0; matrix products, arithmetic and copies ran while one was open for 13% -> 0% of each run, Pallas kernels for 0% -> 0%
where the time goes in v1:
time: 76.1 us; the launch traced here: 76 us
  Pallas kernels  69.7 us (92%)
  local copies, waits for them, and re-layouts  3.39 us (4%)
  other arithmetic  2.19 us (3%)
    pallas_call x1, Pallas kernels, shards(): pl.pallas_call(functools.partial(body, T, S, total_rows), out_shape=(jax....  69.7 us
    reshape x1, other arithmetic, shards(): grad_kernel = gk[:27 * chans].astype(F32).reshape(3, 3, 3, chans, ce)  2.19 us
    unnamed x9, local copies, waits for them, and re-layouts  1.8 us
    slice x1, local copies, waits for them, and re-layouts, shards(): grad_kernel = gk[:27 * chans].astype(F32).reshape(3, 3, 3, chans, ce)  1.59 us

profile of v1, /device:TPU:0, one launch (start us, length us, event | category | flops | bytes accessed | tf_op | source)
XLA Modules:
  0.0 76.0 jit_solution(14191895484919932367)
XLA Ops:
  0.6 69.7 %shard_map.93 = (bf16[1,12,20,256]{3,2,1,0:T(8,128)(2,1)}, bf16[7168,128]{1,0:T(8,128)(2,1)}, f32[1,256]{1,0:T(1,128)}, f32[1,256]{1,0:T(1,128)}) custom-call(bf16[1,12,20,256]{3,2,1,0:T(8,128)(2,1)} %x_ref.1, bf16[1,12,20,256]{3,2,1,0:T(8,128)(2,1)} %co_ref.1, bf16[3,3,3,256,256]{4,3,2,1,0:T(8,128)(2,1)} %k_ref.1, f32[1,256]{1,0:T(1,128)} %bitcast.7, ...), custom_call_target="tpu_custom_call" | custom-call | tf_op jit(solution)/shard_map/pallas_call | solution.py:342
  70.4 1.6 %slice.3 = bf16[6912,128]{1,0:T(8,128)(2,1)S(1)} slice(bf16[7168,128]{1,0:T(8,128)(2,1)} %get-tuple-element.9), slice={[0:6912], [0:128]} | slice | bytes 3538944 | tf_op jit(solution)/shard_map/slice | solution.py:381
  72.0 0.0 copy-start
  72.0 0.0 copy-start.2
  72.0 0.0 copy-start.1
  72.0 2.2 %convert.1 = f32[3,3,3,256,128]{4,3,2,1,0:T(8,128)} convert(bf16[3,3,3,256,128]{4,3,2,1,0:T(8,128)(2,1)S(1)} %bitcast.6) | non-fusion elementwise | flops 884736 | bytes 5308416 | tf_op jit(solution)/shard_map/reshape | solution.py:381
  74.2 0.0 copy-done
  74.2 0.7 copy.13
  74.8 0.0 copy-done.2
  74.8 0.6 copy.14
  75.4 0.0 copy-done.1
  75.4 0.6 copy.15
Async XLA Ops:
  72.0 2.2 %copy-start = (bf16[1,12,20,256]{3,2,1,0:T(8,128)(2,1)S(1)}, bf16[1,12,20,256]{3,2,1,0:T(8,128)(2,1)}, u32[]{:S(2)}) copy-start(bf16[1,12,20,256]{3,2,1,0:T(8,128)(2,1)} %get-tuple-element.16) | copy-start | bytes 368644
  72.0 2.9 %copy-start.2 = (f32[1,256]{1,0:T(1,128)S(1)}, f32[1,256]{1,0:T(1,128)}, u32[]{:S(2)}) copy-start(f32[1,256]{1,0:T(1,128)} %get-tuple-element.10) | copy-start | bytes 3076
  72.0 3.4 %copy-start.1 = (f32[1,256]{1,0:T(1,128)S(1)}, f32[1,256]{1,0:T(1,128)}, u32[]{:S(2)}) copy-start(f32[1,256]{1,0:T(1,128)} %get-tuple-element.11) | copy-start | bytes 3076

commit v2 on v1

--- a/solution.py
+++ b/solution.py
@@ -8,6 +8,8 @@
 from jax.sharding import PartitionSpec as P
 
 GROUPS = 32
+STREAMS = 4
+PARTS = 3
 EPSILON = 1e-06
 MESH = pl.DeviceIdType.MESH
 F32 = jnp.float32
@@ -30,15 +32,26 @@
     return x
 
 
+def hand_out(gi_in, gk_in, gg_in, gb_in, gi_out, gk_out, gg_out, gb_out):
+    gk_out[...] = gk_in[...].astype(F32)
+
+    @pl.when(pl.program_id(0) == 0)
+    def _():
+        gi_out[...] = gi_in[...]
+        gg_out[...] = gg_in[...]
+        gb_out[...] = gb_in[...]
+
+
 def body(
-    T, S, total_rows,
-    x_ref, co_ref, k_ref, gain_ref, bias_ref, ct_ref,
+    T, S, sizes,
+    x_hbm, co_hbm, k_ref, gain_ref, bias_ref, ct_hbm,
     gi_ref, gk_ref, gg_ref, gb_ref,
-    strip, edge_out, edge_in, slice_out, slice_in, x_in,
+    x_ref, co_ref, ct_ref, strip, edge_out, edge_in, slice_out, slice_in, x_in,
     st_out, st_in, fbuf, gown, gwide, xt, wbuf, acc, sbuf, rbuf,
-    w_sem, st_send, st_recv, bulk_send, bulk_recv, rs_send, rs_recv,
+    in_sem, w_sem, st_send, st_recv, bulk_send, bulk_recv, rs_send, rs_recv,
 ):
     N = T * S
+    total_rows = sum(sizes)
     _, rows, cols, chans = co_ref.shape
     ce = chans // S
     pitch = fbuf.shape[1]
@@ -49,6 +62,12 @@
     s = lax.axis_index("space")
     me = t * S + s
 
+    loads = [
+        pltpu.make_async_copy(src, dst, in_sem.at[i])
+        for i, (src, dst) in enumerate(((co_hbm, co_ref), (ct_hbm, ct_ref), (x_hbm, x_ref)))
+    ]
+    for copy in loads:
+        copy.start()
     load = pltpu.make_async_copy(k_ref, wbuf, w_sem)
     load.start()
 
@@ -61,6 +80,8 @@
 
     lax.fori_loop(1, N, greet, 0)
 
+    for copy in loads:
+        copy.wait()
     for arr, ref in ((0, co_ref), (1, ct_ref)):
         whole = ref[0]
         for h in range(rows):
@@ -218,6 +239,61 @@
             for c, w in enumerate(shifts(f)):
                 gwide[r, k, :, c * ce : (c + 1) * ce] = w.astype(BF16)
 
+    bits = T.bit_length() - 1
+    straight = list(range(bits))
+    swapped = list(range(bits))
+    if bits > 2:
+        swapped[1], swapped[2] = swapped[2], swapped[1]
+    streams = len(sizes)
+    orders = [(straight, swapped)[p % 2] for p in range(streams)]
+    bases = [sum(sizes[:p]) for p in range(streams)]
+    offs = [0] * streams
+    flying = [None] * streams
+    copies = []
+
+    def side(bit):
+        return lax.rem(t // (2**bit), 2)
+
+    def partner(bit):
+        return (t + (1 - 2 * side(bit)) * 2**bit, s)
+
+    def span(p, off, n):
+        return pl.ds(pl.multiple_of(bases[p] + off, 16), n)
+
+    def begin(i, p):
+        half = sizes[p] >> (i + 1)
+        start = bases[p] + sizes[p] - (sizes[p] >> i)
+        bit = orders[p][i]
+        mine = side(bit)
+        sbuf[start : start + half, :] = acc[span(p, offs[p] + (1 - mine) * half, half), :].astype(BF16)
+        copy = pltpu.make_async_remote_copy(
+            src_ref=sbuf.at[start : start + half], dst_ref=rbuf.at[start : start + half],
+            send_sem=rs_send.at[0, p, i], recv_sem=rs_recv.at[0, p, i],
+            device_id=partner(bit), device_id_type=MESH,
+        )
+        copy.start()
+        copies.append(copy)
+        offs[p] = offs[p] + mine * half
+        flying[p] = copy
+
+    def finish(i, p):
+        half = sizes[p] >> (i + 1)
+        start = bases[p] + sizes[p] - (sizes[p] >> i)
+        flying[p].wait_recv()
+        at = span(p, offs[p], half)
+        acc[at, :] = acc[at, :] + rbuf[start : start + half, :].astype(F32)
+
+    def input_grad(a, total):
+        for b in range(3):
+            for c in range(3):
+                term = lax.dot_general(
+                    gown[2 - a, (2 - b) * pitch : (2 - b) * pitch + flat, c * chans : (c + 1) * chans],
+                    wbuf[a, b, c], (((1,), (1,)), ((), ())), preferred_element_type=F32,
+                )
+                total = term if total is None else total + term
+        return total
+
+    started = 0
     for a in range(3):
         for b in range(3):
             res = None
@@ -230,76 +306,25 @@
             for c in range(3):
                 at = ((a * 3 + b) * 3 + c) * chans
                 acc[at : at + chans, :] = res[:, c * ce : (c + 1) * ce]
-
-    bits = T.bit_length() - 1
-    orders = [list(range(bits)), list(range(bits))]
-    if bits > 2:
-        orders[1][1], orders[1][2] = orders[1][2], orders[1][1]
-    size = total_rows // 2
-    offs = [0, 0]
-    where = 0
-    copies = []
-
-    def side(bit):
-        return lax.rem(t // (2**bit), 2)
-
-    def partner(bit):
-        return (t + (1 - 2 * side(bit)) * 2**bit, s)
-
-    def span(p, off, n):
-        return pl.ds(pl.multiple_of(p * size + off, 16), n)
-
-    def begin(i, p):
-        half = size >> (i + 1)
-        start = size - (size >> i)
-        bit = orders[p][i]
-        mine = side(bit)
-        sbuf[p, start : start + half, :] = acc[span(p, offs[p] + (1 - mine) * half, half), :].astype(BF16)
-        copy = pltpu.make_async_remote_copy(
-            src_ref=sbuf.at[p, start : start + half], dst_ref=rbuf.at[p, start : start + half],
-            send_sem=rs_send.at[0, p, i], recv_sem=rs_recv.at[0, p, i],
-            device_id=partner(bit), device_id_type=MESH,
-        )
-        copy.start()
-        copies.append(copy)
-        offs[p] = offs[p] + mine * half
-        return copy
-
-    def finish(i, p, copy):
-        half = size >> (i + 1)
-        start = size - (size >> i)
-        copy.wait_recv()
-        at = span(p, offs[p], half)
-        acc[at, :] = acc[at, :] + rbuf[p, start : start + half, :].astype(F32)
-
-    def input_grad(taps):
-        total = None
-        for a, b, c in taps:
-            term = lax.dot_general(
-                gown[2 - a, (2 - b) * pitch : (2 - b) * pitch + flat, c * chans : (c + 1) * chans],
-                wbuf[a, b, c], (((1,), (1,)), ((), ())), preferred_element_type=F32,
-            )
-            total = term if total is None else total + term
-        return total
-
-    flying = [begin(0, 0), begin(0, 1)]
+            done = total_rows if a * 3 + b == 8 else ((a * 3 + b) * 3 + 3) * chans
+            while started < streams and bases[started] + sizes[started] <= done:
+                begin(0, started)
+                started += 1
+
+    load.wait()
+    total = None
     for i in range(bits):
-        for p in range(2):
-            finish(i, p, flying[p])
+        for p in range(streams):
+            finish(i, p)
             if i + 1 < bits:
-                flying[p] = begin(i + 1, p)
+                begin(i + 1, p)
         if i == 0:
-            load.wait()
-            every = [(a, b, c) for a in range(3) for b in range(3) for c in range(3)]
-            total = input_grad(every).reshape(rows, pitch, chans)
-            gi_ref[0] = total[:, 0:cols, :].astype(BF16)
-    block = size >> bits
-    for p in range(2):
-        at = span(p, offs[p], block)
-        gk_ref[at, :] = acc[at, :].astype(BF16)
+            for a in range(3):
+                total = input_grad(a, total)
+            gi_ref[0] = total.reshape(rows, pitch, chans)[:, 0:cols, :].astype(BF16)
 
     def spread(i, p):
-        n = size >> (i + 1)
+        n = sizes[p] >> (i + 1)
         bit = orders[p][i]
         at = span(p, offs[p], n)
         copy = pltpu.make_async_remote_copy(
@@ -310,14 +335,17 @@
         copy.start()
         copies.append(copy)
         offs[p] = offs[p] - side(bit) * n
-        return copy
-
-    flying = [spread(bits - 1, 0), spread(bits - 1, 1)]
+        flying[p] = copy
+
+    for p in range(streams):
+        at = span(p, offs[p], sizes[p] >> bits)
+        gk_ref[at, :] = acc[at, :].astype(BF16)
+        spread(bits - 1, p)
     for i in reversed(range(bits)):
-        for p in range(2):
+        for p in range(streams):
             flying[p].wait_recv()
             if i > 0:
-                flying[p] = spread(i - 1, p)
+                spread(i - 1, p)
 
     for copy in copies:
         copy.wait_send()
@@ -334,22 +362,28 @@
         _, rows, cols, chans = conv_out.shape
         ce = chans // S
         bits = T.bit_length() - 1
-        total_rows = round_up(27 * chans, 2 * T * 16)
+        groups = round_up(27 * chans, T * 16) // (T * 16)
+        streams = min(STREAMS, groups)
+        sizes = [(groups // streams + (p < groups % streams)) * T * 16 for p in range(streams)]
+        total_rows = sum(sizes)
         pitch = round_up(cols + 2, 16)
         n_bulk = 3 * (2 + S - 1) + (S - 1) + 4
-        size = total_rows // 2
         vmem = pl.BlockSpec(memory_space=pltpu.VMEM)
+        whole = pl.BlockSpec(memory_space=pl.ANY)
         gi, gk, gg, gb = pl.pallas_call(
-            functools.partial(body, T, S, total_rows),
+            functools.partial(body, T, S, sizes),
             out_shape=(
                 jax.ShapeDtypeStruct(conv_input.shape, BF16),
                 jax.ShapeDtypeStruct((total_rows, ce), BF16),
                 jax.ShapeDtypeStruct((1, chans), F32),
                 jax.ShapeDtypeStruct((1, chans), F32),
             ),
-            in_specs=[vmem, vmem, pl.BlockSpec(memory_space=pl.ANY), vmem, vmem, vmem],
+            in_specs=[whole, whole, whole, vmem, vmem, whole],
             out_specs=(vmem, vmem, vmem, vmem),
             scratch_shapes=[
+                pltpu.VMEM(conv_input.shape, BF16),
+                pltpu.VMEM(conv_out.shape, BF16),
+                pltpu.VMEM(cotangent.shape, BF16),
                 pltpu.VMEM((2, 2, rows, cols, chans), BF16),
                 pltpu.VMEM((2, 2, rows, chans), BF16),
                 pltpu.VMEM((3, 2, 2, rows, chans), BF16),
@@ -364,22 +398,45 @@
                 pltpu.VMEM((S, chans, rows * pitch), BF16),
                 pltpu.VMEM((3, 3, 3, chans, chans), BF16),
                 pltpu.VMEM((total_rows, ce), F32),
-                pltpu.VMEM((2, size, ce), BF16),
-                pltpu.VMEM((2, size, ce), BF16),
+                pltpu.VMEM((total_rows, ce), BF16),
+                pltpu.VMEM((total_rows, ce), BF16),
+                pltpu.SemaphoreType.DMA((3,)),
                 pltpu.SemaphoreType.DMA,
                 pltpu.SemaphoreType.DMA((2,)),
                 pltpu.SemaphoreType.DMA((2,)),
                 pltpu.SemaphoreType.DMA((n_bulk,)),
                 pltpu.SemaphoreType.DMA((n_bulk,)),
-                pltpu.SemaphoreType.DMA((2, 2, bits)),
-                pltpu.SemaphoreType.DMA((2, 2, bits)),
+                pltpu.SemaphoreType.DMA((2, streams, bits)),
+                pltpu.SemaphoreType.DMA((2, streams, bits)),
             ],
             compiler_params=pltpu.CompilerParams(
                 collective_id=0, has_side_effects=True, vmem_limit_bytes=60 * 1024 * 1024
             ),
         )(conv_input, conv_out, kernel, gain.reshape(1, chans), bias.reshape(1, chans), cotangent)
-        grad_kernel = gk[: 27 * chans].astype(F32).reshape(3, 3, 3, chans, ce)
-        return gi, grad_kernel, gg.reshape(chans), gb.reshape(chans)
+        part_rows = 27 * chans // PARTS
+        gi, gk, gg, gb = pl.pallas_call(
+            hand_out,
+            grid=(PARTS,),
+            out_shape=(
+                jax.ShapeDtypeStruct(gi.shape, BF16),
+                jax.ShapeDtypeStruct((27 * chans, ce), F32),
+                jax.ShapeDtypeStruct((1, chans), F32),
+                jax.ShapeDtypeStruct((1, chans), F32),
+            ),
+            in_specs=[
+                pl.BlockSpec(gi.shape, lambda i: (0, 0, 0, 0)),
+                pl.BlockSpec((part_rows, ce), lambda i: (i, 0)),
+                pl.BlockSpec((1, chans), lambda i: (0, 0)),
+                pl.BlockSpec((1, chans), lambda i: (0, 0)),
+            ],
+            out_specs=(
+                pl.BlockSpec(gi.shape, lambda i: (0, 0, 0, 0)),
+                pl.BlockSpec((part_rows, ce), lambda i: (i, 0)),
+                pl.BlockSpec((1, chans), lambda i: (0, 0)),
+                pl.BlockSpec((1, chans), lambda i: (0, 0)),
+            ),
+        )(gi, gk, gg, gb)
+        return gi, gk.reshape(3, 3, 3, chans, ce), gg.reshape(chans), gb.reshape(chans)
 
     strip = P("tm", None, "space", None)
     return jax.shard_map(

time: 76.1 us -> 67.9 us (0.89)
  local copies, waits for them, and re-layouts: 3.39 us -> 0 us
  Pallas kernels: 69.7 us -> 67 us
  other arithmetic: 2.19 us -> 0 us
    pallas_call x1 -> x2, Pallas kernels: 69.7 us -> 67 us  [the longest x1 63.1 us: shards(): pl.pallas_call(functools.partial(body, T, S, sizes), out_shape=(jax.Shape...]
    reshape x1 -> x0, other arithmetic: 2.19 us -> none  [shards(): grad_kernel = gk[:27 * chans].astype(F32).reshape(3, 3, 3, chans, ce)]
    unnamed x9 -> x0, local copies, waits for them, and re-layouts: 1.8 us -> none
    slice x1 -> x0, local copies, waits for them, and re-layouts: 1.59 us -> none  [shards(): grad_kernel = gk[:27 * chans].astype(F32).reshape(3, 3, 3, chans, ce)]
where the time goes in v2:
time: 67.9 us; the launch traced here: 67.7 us
  Pallas kernels  67 us (99%)
    pallas_call x1, Pallas kernels, shards(): pl.pallas_call(functools.partial(body, T, S, sizes), out_shape=(jax.Shape...  63.1 us
    pallas_call x1, Pallas kernels, shards(): pl.pallas_call(hand_out, grid=(PARTS,), out_shape=(jax.ShapeDtypeStruct(g...  3.9 us

profile of v2, /device:TPU:0, one launch (start us, length us, event | category | flops | bytes accessed | tf_op | source)
XLA Modules:
  0.0 67.7 jit_solution(9748861646505014065)
XLA Ops:
  0.6 63.1 %shard_map.93 = (bf16[1,12,20,256]{3,2,1,0:T(8,128)(2,1)}, bf16[6912,128]{1,0:T(8,128)(2,1)}, f32[1,256]{1,0:T(1,128)}, f32[1,256]{1,0:T(1,128)}) custom-call(bf16[1,12,20,256]{3,2,1,0:T(8,128)(2,1)} %x_hbm.1, bf16[1,12,20,256]{3,2,1,0:T(8,128)(2,1)} %co_hbm.1, bf16[3,3,3,256,256]{4,3,2,1,0:T(8,128)(2,1)} %k_ref.1, f32[1,256]{1,0:T(1,128)} %bitcast.5, ...), custom_call_target="tpu_custom_call" | custom-call | tf_op jit(solution)/shard_map/pallas_call | solution.py:373
  63.8 3.9 %shard_map.94 = (bf16[1,12,20,256]{3,2,1,0:T(8,128)(2,1)}, f32[6912,128]{1,0:T(8,128)}, f32[1,256]{1,0:T(1,128)}, f32[1,256]{1,0:T(1,128)}) custom-call(bf16[1,12,20,256]{3,2,1,0:T(8,128)(2,1)} %get-tuple-element.12.gi_in, bf16[6912,128]{1,0:T(8,128)(2,1)} %get-tuple-element.13.gk_in, f32[1,256]{1,0:T(1,128)} %get-tuple-element.14.gg_in, ...), custom_call_target="tpu_custom_call" | custom-call | tf_op jit(solution)/shard_map/pallas_call | solution.py:417

commit v3 on v2

--- a/solution.py
+++ b/solution.py
@@ -8,8 +8,8 @@
 from jax.sharding import PartitionSpec as P
 
 GROUPS = 32
-STREAMS = 4
-PARTS = 3
+STREAMS = 6
+PARTS = 2
 EPSILON = 1e-06
 MESH = pl.DeviceIdType.MESH
 F32 = jnp.float32
@@ -100,6 +100,7 @@
 
     def send_stats(which):
         def send(r, carry):
+            r = 1 + lax.rem(r + N // 2 - 1, N - 1)
             d = lax.rem(me + r, N)
             pltpu.make_async_remote_copy(
                 src_ref=st_out.at[which], dst_ref=st_in.at[which, r - 1],
@@ -129,19 +130,33 @@
         copy.start()
         bulk.append(copy)
 
+    back = lax.rem(t + T - 1, T)
+    for arr, ref in ((0, co_ref), (1, ct_ref)):
+        push(ref.at[0], strip.at[0, arr], (back, s))
+    for r in range(1, S):
+        other = lax.rem(s + S - r, S)
+        push(slice_out.at[other], slice_in.at[0, r - 1], (t, other))
+    relayed = len(bulk)
     for k in range(3):
         tk = lax.rem(t + T - k, T)
         push(edge_out.at[1], edge_in.at[k, 0], (tk, lax.rem(s + 1, S)))
         push(edge_out.at[0], edge_in.at[k, 1], (tk, lax.rem(s + S - 1, S)))
-        for r in range(1, S):
-            other = lax.rem(s + S - r, S)
-            push(slice_out.at[other], slice_in.at[k, r - 1], (tk, other))
     for r in range(1, S):
         push(x_ref.at[0], x_in.at[r - 1], (t, lax.rem(s + S - r, S)))
-    for k in range(1, 3):
-        tk = lax.rem(t + T - k, T)
-        push(co_ref.at[0], strip.at[k - 1, 0], (tk, s))
-        push(ct_ref.at[0], strip.at[k - 1, 1], (tk, s))
+    direct = len(bulk)
+
+    def relay_first():
+        for arr in range(2):
+            bulk[arr].wait_recv()
+            push(strip.at[0, arr], strip.at[1, arr], (back, s))
+        for r in range(1, S):
+            bulk[1 + r].wait_recv()
+            push(slice_in.at[0, r - 1], slice_in.at[1, r - 1], (back, s))
+
+    def relay_second():
+        for r in range(1, S):
+            bulk[direct + 1 + r].wait_recv()
+            push(slice_in.at[1, r - 1], slice_in.at[2, r - 1], (back, s))
 
     fbuf[...] = jnp.zeros_like(fbuf)
 
@@ -158,6 +173,7 @@
     bias = bias_ref[...]
     width = chans // GROUPS
     count = rows * cols * width * N
+    relay_first()
     sums = take_stats(0)
     grouped = group_sum(sums, width)
     mean2 = grouped[:halves] / count
@@ -181,10 +197,13 @@
         jnp.sum(jnp.sum(grad * normed, axis=0), axis=0, keepdims=True),
     )
     send_stats(1)
-    for copy in bulk:
+    relay_second()
+    for copy in bulk[relayed:direct]:
         copy.wait_recv()
     for r in range(1, S):
         put_input(r, x_in[r - 1])
+    for copy in bulk[direct : direct + 2] + bulk[direct + 1 + S :]:
+        copy.wait_recv()
     sums = take_stats(1)
     chan_bias, chan_gain = wide(sums[:halves]), wide(sums[halves:])
     gb_ref[...] = chan_bias

time: 67.9 us -> 63 us (0.928); the launches traced: 67.7 us -> 61.8 us
  Pallas kernels: 67 us -> 61.1 us
    pallas_call x1, Pallas kernels: 63.1 us -> 58 us  [shards(): pl.pallas_call(functools.partial(body, T, S, sizes), out_shape=(jax.Shape...]
    pallas_call x1, Pallas kernels: 3.9 us -> 3.17 us  [shards(): pl.pallas_call(hand_out, grid=(PARTS,), out_shape=(jax.ShapeDtypeStruct(g...]
where the time goes in v3:
time: 63 us; the launch traced here: 61.8 us
  Pallas kernels  61.1 us (97%)
  between operations  0.64 us (1%)
    pallas_call x1, Pallas kernels, shards(): pl.pallas_call(functools.partial(body, T, S, sizes), out_shape=(jax.Shape...  58 us
    pallas_call x1, Pallas kernels, shards(): pl.pallas_call(hand_out, grid=(PARTS,), out_shape=(jax.ShapeDtypeStruct(g...  3.17 us

profile of v3, /device:TPU:0, one launch (start us, length us, event | category | flops | bytes accessed | tf_op | source)
XLA Modules:
  0.0 61.8 jit_solution(5925131388942344253)
XLA Ops:
  0.6 58.0 %shard_map.93 = (bf16[1,12,20,256]{3,2,1,0:T(8,128)(2,1)}, bf16[6912,128]{1,0:T(8,128)(2,1)}, f32[1,256]{1,0:T(1,128)}, f32[1,256]{1,0:T(1,128)}) custom-call(bf16[1,12,20,256]{3,2,1,0:T(8,128)(2,1)} %x_hbm.1, bf16[1,12,20,256]{3,2,1,0:T(8,128)(2,1)} %co_hbm.1, bf16[3,3,3,256,256]{4,3,2,1,0:T(8,128)(2,1)} %k_ref.1, f32[1,256]{1,0:T(1,128)} %bitcast.5, ...), custom_call_target="tpu_custom_call" | custom-call | tf_op jit(solution)/shard_map/pallas_call | solution.py:392
  58.6 3.2 %shard_map.94 = (bf16[1,12,20,256]{3,2,1,0:T(8,128)(2,1)}, f32[6912,128]{1,0:T(8,128)}, f32[1,256]{1,0:T(1,128)}, f32[1,256]{1,0:T(1,128)}) custom-call(bf16[1,12,20,256]{3,2,1,0:T(8,128)(2,1)} %get-tuple-element.12.gi_in, bf16[6912,128]{1,0:T(8,128)(2,1)} %get-tuple-element.13.gk_in, f32[1,256]{1,0:T(1,128)} %get-tuple-element.14.gg_in, ...), custom_call_target="tpu_custom_call" | custom-call | tf_op jit(solution)/shard_map/pallas_call | solution.py:436
